TPU v7x, 512 devices: a whole 4x4x16 slice. The times are simulated.
512 devices in a mesh: region: 64 (over z, y_hi, core), tracer: 8 (over x, y_lo).
Axes of the slice: x: 4, y: 4 (y_hi: 2, y_lo: 2; y = y_hi * 2 + y_lo), z: 16, core: 2. Of those that a mesh axis runs over, the one named last changes fastest.
Arguments:
- cotangent: float32 [32, 32768], P('tracer', 'region'), may hold values from -6 to 6
- states: float32 [6, 32, 32768], P(None, 'tracer', 'region'), may hold values from -6 to 6
- implicit_inverse: float32 [1024, 32, 32], P('region'), may hold values from -3 to 3
- wet_levels: int32 [1024], P('region'), may hold values from 1 to 32
- explicit_tiles: bfloat16 [64, 5, 512, 512], P('region'), may hold values from -0.125 to 0.125
- tile_offset: int32 [64, 5], P('region'), may hold values from -2 to 2, as said below
- tile_count: int32 [64], P('region'), may hold values from 1 to 5
- uptake_weight: float32 [32, 32], replicated, may hold values from -1 to 1
- release_weight: float32 [32, 32], replicated, may hold values from -1 to 1
Outputs:
- initial_adjoint: float32 [32, 32768], P('tracer', 'region')
Inputs may be any that keep to these rules, and one draw needn't show every extreme that they name: `tile_offset`: the offsets of one region are distinct; only the first tile_count slots of a region are used.
All inputs are finite; a program needn't handle non-finite values.
Results may differ from a plain program's by a relative error of at most 0.0032.
Values sent between devices are 32-bit elements; how exact they have to be, the bound alone decides.
No kernel may reach another device: no remote copies, remote signals or barrier semaphores. Data moves between devices by JAX's collectives and lax.ppermute only.
A program may use at most 64 MiB of HBM per device.

v0:
```python
import jax
import jax.numpy as jnp
from jax import lax
from jax.experimental import pallas as pl
from jax.experimental.pallas import tpu as pltpu
from jax.sharding import Mesh, PartitionSpec as P


REGION = ("z", "yhi", "core")
TRACER = ("x", "ylo")
EVERY = REGION + TRACER
SPAN = 256
VMEM_LIMIT = 8 * 2**20
COUNT_AT, CORE_AT = 5, 6


def neighbour_groups(sizes):
    nq, nx, ny = sizes

    def at(chip, core, x, ylo):
        return (((chip % nq) * 2 + core) * nx + x) * ny + ylo

    groups = []
    for q in range(nq):
        for x in range(nx):
            joined, alone = (1, 0) if q % 2 == 0 else (0, 1)
            groups.append([at(q, 1, x, joined), at(q + 1, 0, x, 1 - joined)])
            groups.append([at(q, 1, x, alone), at(q, 0, x, alone)])
    return groups


def chip_groups(sizes):
    nq, nx, ny = sizes
    return [
        [((q * 2 + core) * nx + x) * ny + ylo for ylo in range(ny) for core in range(2)]
        for q in range(nq)
        for x in range(nx)
    ]


def halves(value):
    high = value.astype(jnp.bfloat16)
    low = (value - high.astype(jnp.float32)).astype(jnp.bfloat16)
    return high, low


def dot(a, b):
    return lax.dot_general(a, b, (((1,), (0,)), ((), ())), preferred_element_type=jnp.float32)


def dot_split(a_high, a_low, b_high, b_low):
    rows = a_high.shape[0]
    both = dot(jnp.concatenate([a_high, a_low], axis=0), b_high)
    return both[:rows] + both[rows:] + dot(a_high, b_low)


def slot_at(offsets, slots, distance):
    slot = jnp.int32(0)
    for k in range(slots):
        slot = slot + jnp.where(offsets[k] == distance, k, 0)
    return slot


def slot_live(offsets, slots, distance):
    live = jnp.int32(0)
    for k in range(slots):
        live = live + jnp.where((offsets[k] == distance) & (k < offsets[COUNT_AT]), 1, 0)
    return live > 0


def pack_kernel(cotangent, states, copies, buffer, fetched):
    first = pltpu.make_async_copy(cotangent, buffer.at[0], fetched.at[0])
    rest = pltpu.make_async_copy(states, buffer.at[pl.ds(1, states.shape[0])], fetched.at[1])
    first.start()
    rest.start()
    first.wait()
    rest.wait()
    for t in range(copies.shape[0]):
        copies[t] = buffer[...]


def lend_kernel(offsets_hbm, tiles, lent, offsets, buffer, arrival):
    ask = pltpu.make_async_copy(offsets_hbm, offsets, arrival.at[0])
    ask.start()
    ask.wait()
    distance = 2 - 4 * lax.axis_index("core")
    fetch = pltpu.make_async_copy(tiles.at[0, slot_at(offsets.at[0], tiles.shape[1], distance)], buffer, arrival.at[1])
    fetch.start()
    fetch.wait()
    lent[...] = buffer[...].astype(jnp.float32)


def arrange_kernel(facts, wet, tiles, inverse, ordered, shared, upper, arrival):
    slots = tiles.shape[1]
    direction = 2 * facts[CORE_AT] - 1
    uses = (direction, 2 * direction, 0, -direction)
    fetches = [
        pltpu.make_async_copy(tiles.at[0, slot_at(facts, slots, distance)], ordered.at[n], arrival.at[n])
        for n, distance in enumerate(uses)
    ]
    for fetch in fetches:
        fetch.start()
    columns, levels, _ = inverse.shape
    lane = lax.broadcasted_iota(jnp.int32, (levels, levels), 1)
    row = lax.broadcasted_iota(jnp.int32, (8, levels), 1)
    for c in range(columns):
        at = slice(c * levels, (c + 1) * levels)
        shared[0:levels, at] = jnp.where(lane < wet[c], inverse[c], 0.0)
        shared[levels : levels + 8, at] = jnp.where(row < wet[c], 1.0, 0.0)
    lending = jnp.where(slot_live(facts, slots, -2 * direction), 1.0, 0.0)
    shared[levels + 4 :, :] = jnp.full((4, shared.shape[1]), lending, jnp.float32)
    upper[...] = jnp.full(upper.shape, facts[CORE_AT], jnp.int32).astype(jnp.float32)
    for fetch in fetches:
        fetch.wait()
    for n, distance in enumerate(uses):

        @pl.when(jnp.logical_not(slot_live(facts, slots, distance)))
        def _():
            ordered[n] = jnp.zeros(ordered.shape[1:], ordered.dtype)


def gathered_kernel(gathered, shared, uptake_weight, start, slopes):
    peers, _, few, _ = gathered.shape
    tracers = uptake_weight.shape[0]
    start[tracers:, :] = shared[...]
    for t in range(peers):
        at = slice(t * few, (t + 1) * few)
        start[at, :] = gathered[t, 0]
        for n in range(slopes.shape[0]):
            slopes[n, at, :] = gathered[t, 1 + n]
    weight_high, weight_low = halves(uptake_weight[...])
    for n in range(slopes.shape[0]):
        state_high, state_low = halves(slopes[n])
        reach = jnp.tanh(dot_split(weight_high, weight_low, state_high, state_low))
        slopes[n] = 1.0 - reach * reach


def lay_out_blocks(adjoint, is_upper, tracers, levels, blocks, wet):
    spans = adjoint.shape[2] // SPAN
    same = (
        lax.broadcasted_iota(jnp.int32, (SPAN, SPAN), 0) // levels
        == lax.broadcasted_iota(jnp.int32, (SPAN, SPAN), 1) // levels
    )
    for side in range(2):

        def rows(at):
            return jnp.where(is_upper, adjoint[1 - side, at, :], adjoint[side, at, :])

        inverses = rows(slice(tracers, tracers + levels))
        for s in range(spans):
            high, low = halves(inverses[:, s * SPAN : (s + 1) * SPAN])
            full_high = jnp.concatenate([high] * (SPAN // levels), axis=0)
            full_low = jnp.concatenate([low] * (SPAN // levels), axis=0)
            blocks[0, side * spans + s] = jnp.where(same, full_high, jnp.zeros_like(full_high))
            blocks[1, side * spans + s] = jnp.where(same, full_low, jnp.zeros_like(full_low))
        wet[side : side + 1, :] = rows(slice(tracers + levels, tracers + levels + 1))
        wet[2 + side : 3 + side, :] = rows(slice(tracers + levels + 4, tracers + levels + 5))


def settle(value, blocks, side):
    spans = value.shape[1] // SPAN
    high, low = halves(value)
    pieces = []
    for s in range(spans):
        at = slice(s * SPAN, (s + 1) * SPAN)
        k = side * spans + s
        pieces.append(dot_split(high[:, at], low[:, at], blocks[0, k], blocks[1, k]))
    return jnp.concatenate(pieces, axis=1)


def step_kernel(adjoint, ordered, borrowed, upper, slopes, uptake_t, release_t, *rest, section, levels, first):
    tracers = uptake_t.shape[0]
    is_upper = upper[0:1, :] > 0.5
    if first:
        send, keep, blocks, wet, tile, buffer, arrival = rest
        fetch = pltpu.make_async_copy(borrowed, buffer, arrival)
        fetch.start()
        lay_out_blocks(adjoint, is_upper, tracers, levels, blocks, wet)
        lower, higher = adjoint[0, 0:tracers, :], adjoint[1, 0:tracers, :]
    else:
        blocks, wet, send, keep = rest
        tile = borrowed
        lower = adjoint[0, 0:tracers, :] + adjoint[1, tracers:, :]
        higher = adjoint[1, 0:tracers, :] + adjoint[0, tracers:, :]
    own, other = jnp.where(is_upper, higher, lower), jnp.where(is_upper, lower, higher)
    if not first:
        own, other = wet[0:1, :] * own, wet[1:2, :] * other
    own_high, own_low = halves(settle(own, blocks, 0))
    other_high = (wet[3:4, :] * settle(other, blocks, 1)).astype(jnp.bfloat16)
    send[tracers:, :] = dot(own_high, ordered[1])
    release_high, release_low = halves(release_t[...])
    pushed = slopes[section] * dot_split(release_high, release_low, own_high, own_low)
    pushed_high, pushed_low = halves(pushed)
    uptake_high, uptake_low = halves(uptake_t[...])
    keep[0:tracers, :] = dot(own_high, ordered[2]) + dot_split(uptake_high, uptake_low, pushed_high, pushed_low)
    keep[tracers:, :] = dot(own_high, ordered[3])
    if first:
        fetch.wait()
        tile[...] = buffer[...].astype(jnp.bfloat16)
    send[0:tracers, :] = dot(own_high, ordered[0]) + dot(other_high, tile[...])


def local(
    cotangent,
    states,
    implicit_inverse,
    wet_levels,
    explicit_tiles,
    tile_offset,
    tile_count,
    uptake_weight,
    release_weight,
    *,
    sizes,
):
    tracers_here, boxes = cotangent.shape
    sections = states.shape[0]
    _, levels, _ = implicit_inverse.shape
    tracers = uptake_weight.shape[0]
    spans = boxes // SPAN
    peers = tracers // tracers_here
    f32, bf16 = jnp.float32, jnp.bfloat16
    shape = jax.ShapeDtypeStruct
    vmem = pl.BlockSpec(memory_space=pltpu.VMEM)
    smem = pl.BlockSpec(memory_space=pltpu.SMEM)
    hbm = pl.BlockSpec(memory_space=pltpu.HBM)
    lean = pltpu.CompilerParams(vmem_limit_bytes=VMEM_LIMIT)
    dma = pltpu.SemaphoreType.DMA
    core_index = lax.axis_index("core")
    core = core_index.astype(jnp.int32).reshape(1)
    ylo_index, ylo_size = lax.axis_index("ylo"), lax.axis_size("ylo")
    groups = neighbour_groups(sizes)

    def in_hbm(array):
        return pltpu.with_memory_space_constraint(array, pltpu.HBM)

    copies = pl.pallas_call(
        pack_kernel,
        in_specs=[hbm] * 2,
        out_specs=vmem,
        out_shape=shape((peers, 1 + sections, tracers_here, boxes), f32),
        scratch_shapes=[pltpu.VMEM((1 + sections, tracers_here, boxes), f32), dma((2,))],
        compiler_params=lean,
        name="pack",
    )(in_hbm(cotangent), in_hbm(states))
    gathered = lax.all_to_all(copies, TRACER, split_axis=0, concat_axis=0, tiled=True)
    facts = jnp.concatenate([tile_offset.reshape(-1), tile_count, core])
    lent = pl.pallas_call(
        lend_kernel,
        in_specs=[hbm] * 2,
        out_specs=vmem,
        out_shape=shape((boxes, boxes), f32),
        scratch_shapes=[pltpu.SMEM(tile_offset.shape, jnp.int32), pltpu.VMEM((boxes, boxes), bf16), dma((2,))],
        compiler_params=lean,
        name="lend",
    )(in_hbm(tile_offset), in_hbm(explicit_tiles))
    borrowed = in_hbm(lax.ppermute(lent, "core", [(0, 1), (1, 0)]))
    ordered, shared, upper = pl.pallas_call(
        arrange_kernel,
        in_specs=[smem] * 2 + [hbm, vmem],
        out_specs=[vmem] * 3,
        out_shape=[
            shape((4, boxes, boxes), bf16),
            shape((levels + 8, boxes), f32),
            shape((8, boxes), f32),
        ],
        scratch_shapes=[dma((4,))],
        compiler_params=lean,
        name="arrange",
    )(facts, wet_levels, in_hbm(explicit_tiles), implicit_inverse)
    start, slopes = pl.pallas_call(
        gathered_kernel,
        in_specs=[vmem] * 3,
        out_specs=[vmem] * 2,
        out_shape=[shape((tracers + levels + 8, boxes), f32), shape((sections, tracers, boxes), f32)],
        compiler_params=lean,
        name="gathered",
    )(gathered, shared, uptake_weight)
    adjoint = lax.all_gather(start, "core")
    uptake_t, release_t = uptake_weight.T, release_weight.T
    kept_shapes = [shape((2, 2 * spans, SPAN, SPAN), bf16), shape((4, boxes), f32)]
    kept = []
    for section in range(sections - 1, -1, -1):
        first = section == sections - 1

        def step(*refs, section=section, first=first):
            step_kernel(*refs, section=section, levels=levels, first=first)

        out_shape = [shape((2 * tracers, boxes), f32)] * 2 + (kept_shapes + [shape((boxes, boxes), bf16)]) * first
        send, keep, *made = pl.pallas_call(
            step,
            in_specs=[vmem] * 2 + [hbm if first else vmem] + [vmem] * (4 + len(kept)),
            out_specs=[vmem] * len(out_shape),
            out_shape=out_shape,
            scratch_shapes=[pltpu.VMEM((boxes, boxes), f32), dma] * first,
            compiler_params=lean,
        )(adjoint, ordered, borrowed, upper, slopes, uptake_t, release_t, *kept)
        if first:
            *kept, borrowed = made
        if section == 0:
            rows = ylo_size * tracers_here
            at = (0, lax.axis_index("x") * rows, 0)
            send, keep = (
                lax.dynamic_slice(part.reshape(2, tracers, boxes), at, (2, rows, boxes)).reshape(2 * rows, boxes)
                for part in (send, keep)
            )
        arrived = lax.all_gather(send, EVERY, axis_index_groups=groups)
        keep = keep + lax.dynamic_index_in_dim(arrived, core_index, 0, keepdims=False)
        if section > 0:
            adjoint = lax.all_gather(keep, "core")
    final = lax.all_gather(keep, EVERY, axis_index_groups=chip_groups(sizes))
    joined = 2 * (1 - lax.axis_index("yhi"))
    row = ylo_index * tracers_here
    mine = lax.dynamic_slice(final, (joined + core_index, row, 0), (1, tracers_here, boxes))[0]
    theirs = lax.dynamic_slice(final, (joined + 1 - core_index, rows + row, 0), (1, tracers_here, boxes))[0]
    return kept[1][0:1] * (mine + theirs)


def solution(mesh):
    regions, tracer_devices = mesh.devices.shape
    nq, nx, ny = regions // 2, tracer_devices // 2, 2
    fine = Mesh(mesh.devices.reshape(nq // 2, 2, 2, nx, ny), EVERY)
    placed = (
        P(TRACER, REGION),
        P(None, TRACER, REGION),
        P(REGION, None, None),
        P(REGION),
        P(REGION, None, None, None),
        P(REGION, None),
        P(REGION),
        P(),
        P(),
    )

    def body(*args):
        return local(*args, sizes=(nq, nx, ny))

    return jax.shard_map(body, mesh=fine, in_specs=placed, out_specs=P(TRACER, REGION), check_vma=False)
```

profile of v0, /device:TPU:1, one launch (start us, length us, event | category | flops | bytes accessed | tf_op | source)
XLA Modules:
  0.0 95.0 jit_solution(11563327612986887065)
XLA Ops:
  0.0 0.0 copy-start.4
  0.0 0.0 copy-start.1
  0.0 0.0 copy-start.3
  0.0 0.0 copy-start
  0.0 0.0 copy-start.2
  0.0 2.9 %lend.1 = f32[512,512]{1,0:T(8,128)} custom-call(s32[1,5]{1,0:T(1,128)} %offsets_hbm.1, bf16[1,5,512,512]{3,2,1,0:T(8,128)(2,1)} %tiles.3), custom_call_target="tpu_custom_call" | custom-call | tf_op jit(solution)/shard_map/lend/pallas_call | solution.py:248
  3.0 8.7 %collective-permute-start = (f32[512,512]{1,0:T(8,128)}, f32[512,512]{1,0:T(8,128)}, u32[]{:S(2)}, u32[]{:S(2)}) collective-permute-start(f32[512,512]{1,0:T(8,128)} %lend.1), channel_id=1, source_target_pairs={{0,8},{8,0},{1,9},{9,1},{2,10},{10,2},{3,11},{11,3},{4,12},{12,4},... | collective-permute-start | bytes 3145736 | tf_op jit(solution)/shard_map/ppermute | solution.py:257
  11.7 1.6 %pack.1 = f32[8,7,4,512]{3,2,1,0:T(4,128)} custom-call(f32[4,512]{1,0:T(4,128)} %cotangent.1, f32[6,4,512]{2,1,0:T(4,128)} %states.1), custom_call_target="tpu_custom_call" | custom-call | tf_op jit(solution)/shard_map/pack/pallas_call | solution.py:237
  13.3 3.5 %all-to-all-start = ((f32[8,7,4,512]{3,2,1,0:T(4,128)}), f32[8,7,4,512]{3,2,1,0:T(4,128)S(1)}, u32[]{:S(2)}, u32[]{:S(2)}) async-start(f32[8,7,4,512]{3,2,1,0:T(4,128)} %pack.1), calls=%async_computation | async-start | bytes 917504 | tf_op jit(solution)/shard_map/all_to_all | solution.py:246
  17.5 0.0 copy-done.1
  17.5 0.1 copy.12
  17.6 0.0 copy-done.3
  17.6 0.1 copy.13
  17.6 0.0 copy-done.4
  17.6 0.1 pad_add_fusion.facts
  17.7 0.0 copy-done
  17.7 0.0 copy-done.2
  17.7 2.3 %arrange.1 = (bf16[4,512,512]{2,1,0:T(8,128)(2,1)S(1)}, f32[40,512]{1,0:T(8,128)S(1)}, f32[8,512]{1,0:T(8,128)S(1)}) custom-call(s32[7]{0:T(128)S(1)} %pad_add_fusion.facts, s32[16]{0:T(128)S(1)} %copy-done.2, bf16[1,5,512,512]{3,2,1,0:T(8,128)(2,1)} %tiles.3, f32[16,32,32]{2,1,0:T(8,128)S(1)} %copy-done), custom_call_target="tpu_custom_call" | custom-call | tf_op jit(solution)/shard_map/arrange/pallas_call | solution.py:258
  20.0 5.6 %all-to-all-done.gathered = f32[8,7,4,512]{3,2,1,0:T(4,128)S(1)} async-done(((f32[8,7,4,512]{3,2,1,0:T(4,128)}), f32[8,7,4,512]{3,2,1,0:T(4,128)S(1)}, u32[]{:S(2)}, u32[]{:S(2)}) %all-to-all-start) | async-done | bytes 458784 | tf_op jit(solution)/shard_map/all_to_all | solution.py:246
  25.6 0.3 gathered.1
  25.9 2.5 %all-gather = f32[144,512]{1,0:T(8,128)S(1)} all-gather(f32[72,512]{1,0:T(8,128)S(1)} %get-tuple-element.26), channel_id=2, replica_groups=mesh['z'=16,'yhi'=2,'core'=2,'x'=4,'ylo'=2] {'core'}, dimensions={0}, use_global_device_ids=true | all-gather | bytes 442368 | tf_op jit(solution)/shard_map/all_gather | solution.py:279
  28.5 0.0 collective-permute-done.refs_2_
  28.5 1.5 %shard_map.91 = (f32[64,512]{1,0:T(8,128)S(1)}, f32[64,512]{1,0:T(8,128)S(1)}, bf16[2,4,256,256]{3,2,1,0:T(8,128)(2,1)S(1)}, f32[4,512]{1,0:T(4,128)S(1)}, bf16[512,512]{1,0:T(8,128)(2,1)S(1)}) custom-call(f32[2,72,512]{2,1,0:T(8,128)S(1)} %bitcast.34, bf16[4,512,512]{2,1,0:T(8,128)(2,1)S(1)} %get-tuple-element.27.refs_1_, ...), custom_call_target="tpu_custom_call" | custom-call | tf_op jit(solution)/shard_map/pallas_call | solution.py:290
  30.0 2.0 %all-gather.1 = f32[128,512]{1,0:T(8,128)S(1)} all-gather(f32[64,512]{1,0:T(8,128)S(1)} %get-tuple-element.32), channel_id=3, replica_groups={{9,16},{8,0},{11,18},{10,2},{13,20},{12,4},{15,22},{14,6},{24,33},{25,1..., dimensions={0}, use_global_device_ids=true | all-gather | bytes 393216 | tf_op jit(solution)/shard_map/all_gather | solution.py:307
  32.0 2.0 %all-gather.2 = f32[128,512]{1,0:T(8,128)S(1)} all-gather(f32[64,512]{1,0:T(8,128)S(1)} %bitcast_add_fusion.4), channel_id=4, replica_groups=mesh['z'=16,'yhi'=2,'core'=2,'x'=4,'ylo'=2] {'core'}, dimensions={0}, use_global_device_ids=true | all-gather | bytes 393216 | tf_op jit(solution)/shard_map/all_gather | solution.py:310
  34.0 0.9 shard_map.92
  34.9 2.0 %all-gather.3 = f32[128,512]{1,0:T(8,128)S(1)} all-gather(f32[64,512]{1,0:T(8,128)S(1)} %get-tuple-element.36), channel_id=5, replica_groups={{9,16},{8,0},{11,18},{10,2},{13,20},{12,4},{15,22},{14,6},{24,33},{25,1..., dimensions={0}, use_global_device_ids=true | all-gather | bytes 393216 | tf_op jit(solution)/shard_map/all_gather | solution.py:307
  36.9 2.0 %all-gather.4 = f32[128,512]{1,0:T(8,128)S(1)} all-gather(f32[64,512]{1,0:T(8,128)S(1)} %bitcast_add_fusion.3), channel_id=6, replica_groups=mesh['z'=16,'yhi'=2,'core'=2,'x'=4,'ylo'=2] {'core'}, dimensions={0}, use_global_device_ids=true | all-gather | bytes 393216 | tf_op jit(solution)/shard_map/all_gather | solution.py:310
  38.9 0.9 shard_map.93
  39.8 2.0 %all-gather.5 = f32[128,512]{1,0:T(8,128)S(1)} all-gather(f32[64,512]{1,0:T(8,128)S(1)} %get-tuple-element.38), channel_id=7, replica_groups={{9,16},{8,0},{11,18},{10,2},{13,20},{12,4},{15,22},{14,6},{24,33},{25,1..., dimensions={0}, use_global_device_ids=true | all-gather | bytes 393216 | tf_op jit(solution)/shard_map/all_gather | solution.py:307
  41.9 2.0 %all-gather.6 = f32[128,512]{1,0:T(8,128)S(1)} all-gather(f32[64,512]{1,0:T(8,128)S(1)} %bitcast_add_fusion.2), channel_id=8, replica_groups=mesh['z'=16,'yhi'=2,'core'=2,'x'=4,'ylo'=2] {'core'}, dimensions={0}, use_global_device_ids=true | all-gather | bytes 393216 | tf_op jit(solution)/shard_map/all_gather | solution.py:310
  43.8 0.9 shard_map.94
  44.7 2.0 %all-gather.7 = f32[128,512]{1,0:T(8,128)S(1)} all-gather(f32[64,512]{1,0:T(8,128)S(1)} %get-tuple-element.40), channel_id=9, replica_groups={{9,16},{8,0},{11,18},{10,2},{13,20},{12,4},{15,22},{14,6},{24,33},{25,1..., dimensions={0}, use_global_device_ids=true | all-gather | bytes 393216 | tf_op jit(solution)/shard_map/all_gather | solution.py:307
  46.8 2.0 %all-gather.8 = f32[128,512]{1,0:T(8,128)S(1)} all-gather(f32[64,512]{1,0:T(8,128)S(1)} %bitcast_add_fusion.1), channel_id=10, replica_groups=mesh['z'=16,'yhi'=2,'core'=2,'x'=4,'ylo'=2] {'core'}, dimensions={0}, use_global_device_ids=true | all-gather | bytes 393216 | tf_op jit(solution)/shard_map/all_gather | solution.py:310
  48.8 0.9 shard_map.95
  49.7 2.0 %all-gather.9 = f32[128,512]{1,0:T(8,128)S(1)} all-gather(f32[64,512]{1,0:T(8,128)S(1)} %get-tuple-element.42), channel_id=11, replica_groups={{9,16},{8,0},{11,18},{10,2},{13,20},{12,4},{15,22},{14,6},{24,33},{25,1..., dimensions={0}, use_global_device_ids=true | all-gather | bytes 393216 | tf_op jit(solution)/shard_map/all_gather | solution.py:307
  51.7 2.0 %all-gather.10 = f32[128,512]{1,0:T(8,128)S(1)} all-gather(f32[64,512]{1,0:T(8,128)S(1)} %bitcast_add_fusion), channel_id=12, replica_groups=mesh['z'=16,'yhi'=2,'core'=2,'x'=4,'ylo'=2] {'core'}, dimensions={0}, use_global_device_ids=true | all-gather | bytes 393216 | tf_op jit(solution)/shard_map/all_gather | solution.py:310
  53.7 0.9 shard_map.96
  54.6 1.9 %all_gather.95 = f32[2,16,512]{2,1,0:T(8,128)S(1)} all-gather(f32[1,16,512]{2,1,0:T(8,128)S(1)} %dynamic-slice_bitcast_fusion), channel_id=1, replica_groups={{9,16},{8,0},{11,18},{10,2},{13,20},{12,4},{15,22},{14,6},{24,33},{25,1..., dimensions={0}, use_global_device_ids=true | all-gather | bytes 98304 | tf_op jit(solution)/shard_map/all_gather | solution.py:307
  56.5 37.9 %all_gather.96 = f32[4,16,512]{2,1,0:T(8,128)S(1)} all-gather(f32[1,16,512]{2,1,0:T(8,128)S(1)} %bitcast_add_fusion.5), channel_id=1, replica_groups={{0,8,1,9},{2,10,3,11},{4,12,5,13},{6,14,7,15},{16,24,17,25},{18,26,19,2..., dimensions={0}, use_global_device_ids=true | all-gather | bytes 163840 | tf_op jit(solution)/shard_map/all_gather | solution.py:311
  94.4 0.6 bitcast_multiply_fusion
  (8 shorter events, 0.1 us)
Async XLA Ops:
  0.0 17.6 %copy-start.4 = (s32[1,5]{1,0:T(1,128)S(1)}, s32[1,5]{1,0:T(1,128)}, u32[]{:S(2)}) copy-start(s32[1,5]{1,0:T(1,128)} %offsets_hbm.1) | copy-start | bytes 64
  0.0 17.5 %copy-start.1 = (f32[32,32]{1,0:T(8,128)S(1)}, f32[32,32]{1,0:T(8,128)}, u32[]{:S(2)}) copy-start(f32[32,32]{1,0:T(8,128)} %uptake_weight.1) | copy-start | bytes 12292
  0.0 17.6 %copy-start.3 = (f32[32,32]{1,0:T(8,128)S(1)}, f32[32,32]{1,0:T(8,128)}, u32[]{:S(2)}) copy-start(f32[32,32]{1,0:T(8,128)} %param.17) | copy-start | bytes 12292
  0.0 17.7 %copy-start = (f32[16,32,32]{2,1,0:T(8,128)S(1)}, f32[16,32,32]{2,1,0:T(8,128)}, u32[]{:S(2)}) copy-start(f32[16,32,32]{2,1,0:T(8,128)} %inverse.1) | copy-start | bytes 196612
  0.0 17.7 %copy-start.2 = (s32[16]{0:T(128)S(1)}, s32[16]{0:T(128)}, u32[]{:S(2)}) copy-start(s32[16]{0:T(128)} %wet.1) | copy-start | bytes 196
  3.0 25.5 %collective-permute-start = (f32[512,512]{1,0:T(8,128)}, f32[512,512]{1,0:T(8,128)}, u32[]{:S(2)}, u32[]{:S(2)}) collective-permute-start(f32[512,512]{1,0:T(8,128)} %lend.1), channel_id=1, source_target_pairs={{0,8},{8,0},{1,9},{9,1},{2,10},{10,2},{3,11},{11,3},{4,12},{12,4},... | collective-permute-start | bytes 3145736 | tf_op jit(solution)/shard_map/ppermute | solution.py:257
  13.3 12.3 %all-to-all-start = ((f32[8,7,4,512]{3,2,1,0:T(4,128)}), f32[8,7,4,512]{3,2,1,0:T(4,128)S(1)}, u32[]{:S(2)}, u32[]{:S(2)}) async-start(f32[8,7,4,512]{3,2,1,0:T(4,128)} %pack.1), calls=%async_computation | async-start | bytes 917504 | tf_op jit(solution)/shard_map/all_to_all | solution.py:246
where the time goes:
time: 95.5 us; the launch traced here: 95 us
  blocking collectives  62.3 us (65%)
  Pallas kernels  13.2 us (14%)
  starting transfers between devices  12.2 us (13%)
  waiting for transfers between devices  5.6 us (6%)
    all_gather x1, blocking collectives, local(): final = lax.all_gather(keep, EVERY, axis_index_groups=chip_groups(sizes))  37.9 us
    all_gather x6, blocking collectives, local(): arrived = lax.all_gather(send, EVERY, axis_index_groups=groups)  11.9 us
    all_gather x5, blocking collectives, local(): adjoint = lax.all_gather(keep, 'core')  9.97 us
    ppermute x1, starting transfers between devices, local(): borrowed = in_hbm(lax.ppermute(lent, 'core', [(0, 1), (1, 0)]))  8.73 us
    pallas_call x6, Pallas kernels, local(): pl.pallas_call(step, in_specs=[vmem] * 2 + [hbm if first else vmem] + [vm...  6.02 us
    all_to_all x1, waiting for transfers between devices, local(): lax.all_to_all(copies, TRACER, split_axis=0, concat_axis=0, tiled=True)  5.6 us
    all_to_all x1, starting transfers between devices, local(): lax.all_to_all(copies, TRACER, split_axis=0, concat_axis=0, tiled=True)  3.48 us
    pallas_call x1, Pallas kernels, local(): pl.pallas_call(lend_kernel, in_specs=[hbm] * 2, out_specs=vmem, out_shape...  2.91 us
  transfers between devices with their start and end apart: 2, of which 1 were waited for; matrix products, arithmetic and copies ran while one was open for 0% of the time, Pallas kernels for 4%

commit v1 on v0

--- a/solution.py
+++ b/solution.py
@@ -79,15 +79,24 @@
         copies[t] = buffer[...]
 
 
-def lend_kernel(offsets_hbm, tiles, lent, offsets, buffer, arrival):
-    ask = pltpu.make_async_copy(offsets_hbm, offsets, arrival.at[0])
+def in_parts(source, target, arrival):
+    parts = arrival.shape[0]
+    rows = target.shape[0] // parts
+    ats = [pl.ds(n * rows, rows) for n in range(parts)]
+    return [(pltpu.make_async_copy(source.at[at], target.at[at], arrival.at[n]), at) for n, at in enumerate(ats)]
+
+
+def lend_kernel(offsets_hbm, tiles, lent, offsets, buffer, asked, arrival):
+    ask = pltpu.make_async_copy(offsets_hbm, offsets, asked)
     ask.start()
     ask.wait()
     distance = 2 - 4 * lax.axis_index("core")
-    fetch = pltpu.make_async_copy(tiles.at[0, slot_at(offsets.at[0], tiles.shape[1], distance)], buffer, arrival.at[1])
-    fetch.start()
-    fetch.wait()
-    lent[...] = buffer[...].astype(jnp.float32)
+    fetches = in_parts(tiles.at[0, slot_at(offsets.at[0], tiles.shape[1], distance)], buffer, arrival)
+    for fetch, _ in fetches:
+        fetch.start()
+    for fetch, at in fetches:
+        fetch.wait()
+        lent[at, :] = buffer[at, :].astype(jnp.float32)
 
 
 def arrange_kernel(facts, wet, tiles, inverse, ordered, shared, upper, arrival):
@@ -173,8 +182,9 @@
     is_upper = upper[0:1, :] > 0.5
     if first:
         send, keep, blocks, wet, tile, buffer, arrival = rest
-        fetch = pltpu.make_async_copy(borrowed, buffer, arrival)
-        fetch.start()
+        fetches = in_parts(borrowed, buffer, arrival)
+        for fetch, _ in fetches:
+            fetch.start()
         lay_out_blocks(adjoint, is_upper, tracers, levels, blocks, wet)
         lower, higher = adjoint[0, 0:tracers, :], adjoint[1, 0:tracers, :]
     else:
@@ -195,8 +205,9 @@
     keep[0:tracers, :] = dot(own_high, ordered[2]) + dot_split(uptake_high, uptake_low, pushed_high, pushed_low)
     keep[tracers:, :] = dot(own_high, ordered[3])
     if first:
-        fetch.wait()
-        tile[...] = buffer[...].astype(jnp.bfloat16)
+        for fetch, at in fetches:
+            fetch.wait()
+            tile[at, :] = buffer[at, :].astype(jnp.bfloat16)
     send[0:tracers, :] = dot(own_high, ordered[0]) + dot(other_high, tile[...])
 
 
@@ -250,7 +261,7 @@
         in_specs=[hbm] * 2,
         out_specs=vmem,
         out_shape=shape((boxes, boxes), f32),
-        scratch_shapes=[pltpu.SMEM(tile_offset.shape, jnp.int32), pltpu.VMEM((boxes, boxes), bf16), dma((2,))],
+        scratch_shapes=[pltpu.SMEM(tile_offset.shape, jnp.int32), pltpu.VMEM((boxes, boxes), bf16), dma, dma((4,))],
         compiler_params=lean,
         name="lend",
     )(in_hbm(tile_offset), in_hbm(explicit_tiles))
@@ -292,7 +303,7 @@
             in_specs=[vmem] * 2 + [hbm if first else vmem] + [vmem] * (4 + len(kept)),
             out_specs=[vmem] * len(out_shape),
             out_shape=out_shape,
-            scratch_shapes=[pltpu.VMEM((boxes, boxes), f32), dma] * first,
+            scratch_shapes=[pltpu.VMEM((boxes, boxes), f32), dma((4,))] * first,
             compiler_params=lean,
         )(adjoint, ordered, borrowed, upper, slopes, uptake_t, release_t, *kept)
         if first:

time: 95.5 us -> 95.5 us (level)
  no operation moved by 1% of the time
where the time goes in v1:
time: 95.5 us; the launch traced here: 95 us
  blocking collectives  62.3 us (65%)
  Pallas kernels  13.2 us (14%)
  starting transfers between devices  12.2 us (13%)
  waiting for transfers between devices  5.6 us (6%)
    all_gather x1, blocking collectives, local(): final = lax.all_gather(keep, EVERY, axis_index_groups=chip_groups(sizes))  37.9 us
    all_gather x6, blocking collectives, local(): arrived = lax.all_gather(send, EVERY, axis_index_groups=groups)  11.9 us
    all_gather x5, blocking collectives, local(): adjoint = lax.all_gather(keep, 'core')  9.97 us
    ppermute x1, starting transfers between devices, local(): borrowed = in_hbm(lax.ppermute(lent, 'core', [(0, 1), (1, 0)]))  8.73 us
    pallas_call x6, Pallas kernels, local(): pl.pallas_call(step, in_specs=[vmem] * 2 + [hbm if first else vmem] + [vm...  6.04 us
    all_to_all x1, waiting for transfers between devices, local(): lax.all_to_all(copies, TRACER, split_axis=0, concat_axis=0, tiled=True)  5.6 us
    all_to_all x1, starting transfers between devices, local(): lax.all_to_all(copies, TRACER, split_axis=0, concat_axis=0, tiled=True)  3.48 us
    pallas_call x1, Pallas kernels, local(): pl.pallas_call(lend_kernel, in_specs=[hbm] * 2, out_specs=vmem, out_shape...  2.94 us
  transfers between devices with their start and end apart: 2, of which 1 were waited for; matrix products, arithmetic and copies ran while one was open for 0% of the time, Pallas kernels for 4%

profile of v1, /device:TPU:1, one launch (start us, length us, event | category | flops | bytes accessed | tf_op | source)
XLA Modules:
  0.0 95.0 jit_solution(14964457804245003754)
XLA Ops:
  0.0 0.0 copy-start.4
  0.0 0.0 copy-start.1
  0.0 0.0 copy-start.3
  0.0 0.0 copy-start
  0.0 0.0 copy-start.2
  0.0 2.9 %lend.1 = f32[512,512]{1,0:T(8,128)} custom-call(s32[1,5]{1,0:T(1,128)} %offsets_hbm.1, bf16[1,5,512,512]{3,2,1,0:T(8,128)(2,1)} %tiles.3), custom_call_target="tpu_custom_call" | custom-call | tf_op jit(solution)/shard_map/lend/pallas_call | solution.py:259
  3.0 8.7 %collective-permute-start = (f32[512,512]{1,0:T(8,128)}, f32[512,512]{1,0:T(8,128)}, u32[]{:S(2)}, u32[]{:S(2)}) collective-permute-start(f32[512,512]{1,0:T(8,128)} %lend.1), channel_id=1, source_target_pairs={{0,8},{8,0},{1,9},{9,1},{2,10},{10,2},{3,11},{11,3},{4,12},{12,4},... | collective-permute-start | bytes 3145736 | tf_op jit(solution)/shard_map/ppermute | solution.py:268
  11.7 1.6 %pack.1 = f32[8,7,4,512]{3,2,1,0:T(4,128)} custom-call(f32[4,512]{1,0:T(4,128)} %cotangent.1, f32[6,4,512]{2,1,0:T(4,128)} %states.1), custom_call_target="tpu_custom_call" | custom-call | tf_op jit(solution)/shard_map/pack/pallas_call | solution.py:248
  13.4 3.5 %all-to-all-start = ((f32[8,7,4,512]{3,2,1,0:T(4,128)}), f32[8,7,4,512]{3,2,1,0:T(4,128)S(1)}, u32[]{:S(2)}, u32[]{:S(2)}) async-start(f32[8,7,4,512]{3,2,1,0:T(4,128)} %pack.1), calls=%async_computation | async-start | bytes 917504 | tf_op jit(solution)/shard_map/all_to_all | solution.py:257
  17.5 0.0 copy-done.1
  17.5 0.1 copy.12
  17.6 0.0 copy-done.3
  17.6 0.1 copy.13
  17.7 0.0 copy-done.4
  17.7 0.1 pad_add_fusion.facts
  17.8 0.0 copy-done
  17.8 0.0 copy-done.2
  17.8 2.3 %arrange.1 = (bf16[4,512,512]{2,1,0:T(8,128)(2,1)S(1)}, f32[40,512]{1,0:T(8,128)S(1)}, f32[8,512]{1,0:T(8,128)S(1)}) custom-call(s32[7]{0:T(128)S(1)} %pad_add_fusion.facts, s32[16]{0:T(128)S(1)} %copy-done.2, bf16[1,5,512,512]{3,2,1,0:T(8,128)(2,1)} %tiles.3, f32[16,32,32]{2,1,0:T(8,128)S(1)} %copy-done), custom_call_target="tpu_custom_call" | custom-call | tf_op jit(solution)/shard_map/arrange/pallas_call | solution.py:269
  20.0 5.6 %all-to-all-done.gathered = f32[8,7,4,512]{3,2,1,0:T(4,128)S(1)} async-done(((f32[8,7,4,512]{3,2,1,0:T(4,128)}), f32[8,7,4,512]{3,2,1,0:T(4,128)S(1)}, u32[]{:S(2)}, u32[]{:S(2)}) %all-to-all-start) | async-done | bytes 458784 | tf_op jit(solution)/shard_map/all_to_all | solution.py:257
  25.6 0.3 gathered.1
  26.0 2.5 %all-gather = f32[144,512]{1,0:T(8,128)S(1)} all-gather(f32[72,512]{1,0:T(8,128)S(1)} %get-tuple-element.26), channel_id=2, replica_groups=mesh['z'=16,'yhi'=2,'core'=2,'x'=4,'ylo'=2] {'core'}, dimensions={0}, use_global_device_ids=true | all-gather | bytes 442368 | tf_op jit(solution)/shard_map/all_gather | solution.py:290
  28.5 0.0 collective-permute-done.refs_2_
  28.5 1.6 %shard_map.91 = (f32[64,512]{1,0:T(8,128)S(1)}, f32[64,512]{1,0:T(8,128)S(1)}, bf16[2,4,256,256]{3,2,1,0:T(8,128)(2,1)S(1)}, f32[4,512]{1,0:T(4,128)S(1)}, bf16[512,512]{1,0:T(8,128)(2,1)S(1)}) custom-call(f32[2,72,512]{2,1,0:T(8,128)S(1)} %bitcast.34, bf16[4,512,512]{2,1,0:T(8,128)(2,1)S(1)} %get-tuple-element.27.refs_1_, ...), custom_call_target="tpu_custom_call" | custom-call | tf_op jit(solution)/shard_map/pallas_call | solution.py:301
  30.1 2.0 %all-gather.1 = f32[128,512]{1,0:T(8,128)S(1)} all-gather(f32[64,512]{1,0:T(8,128)S(1)} %get-tuple-element.32), channel_id=3, replica_groups={{9,16},{8,0},{11,18},{10,2},{13,20},{12,4},{15,22},{14,6},{24,33},{25,1..., dimensions={0}, use_global_device_ids=true | all-gather | bytes 393216 | tf_op jit(solution)/shard_map/all_gather | solution.py:318
  32.1 2.0 %all-gather.2 = f32[128,512]{1,0:T(8,128)S(1)} all-gather(f32[64,512]{1,0:T(8,128)S(1)} %bitcast_add_fusion.4), channel_id=4, replica_groups=mesh['z'=16,'yhi'=2,'core'=2,'x'=4,'ylo'=2] {'core'}, dimensions={0}, use_global_device_ids=true | all-gather | bytes 393216 | tf_op jit(solution)/shard_map/all_gather | solution.py:321
  34.1 0.9 shard_map.92
  35.0 2.0 %all-gather.3 = f32[128,512]{1,0:T(8,128)S(1)} all-gather(f32[64,512]{1,0:T(8,128)S(1)} %get-tuple-element.36), channel_id=5, replica_groups={{9,16},{8,0},{11,18},{10,2},{13,20},{12,4},{15,22},{14,6},{24,33},{25,1..., dimensions={0}, use_global_device_ids=true | all-gather | bytes 393216 | tf_op jit(solution)/shard_map/all_gather | solution.py:318
  37.0 2.0 %all-gather.4 = f32[128,512]{1,0:T(8,128)S(1)} all-gather(f32[64,512]{1,0:T(8,128)S(1)} %bitcast_add_fusion.3), channel_id=6, replica_groups=mesh['z'=16,'yhi'=2,'core'=2,'x'=4,'ylo'=2] {'core'}, dimensions={0}, use_global_device_ids=true | all-gather | bytes 393216 | tf_op jit(solution)/shard_map/all_gather | solution.py:321
  39.0 0.9 shard_map.93
  39.9 2.0 %all-gather.5 = f32[128,512]{1,0:T(8,128)S(1)} all-gather(f32[64,512]{1,0:T(8,128)S(1)} %get-tuple-element.38), channel_id=7, replica_groups={{9,16},{8,0},{11,18},{10,2},{13,20},{12,4},{15,22},{14,6},{24,33},{25,1..., dimensions={0}, use_global_device_ids=true | all-gather | bytes 393216 | tf_op jit(solution)/shard_map/all_gather | solution.py:318
  41.9 2.0 %all-gather.6 = f32[128,512]{1,0:T(8,128)S(1)} all-gather(f32[64,512]{1,0:T(8,128)S(1)} %bitcast_add_fusion.2), channel_id=8, replica_groups=mesh['z'=16,'yhi'=2,'core'=2,'x'=4,'ylo'=2] {'core'}, dimensions={0}, use_global_device_ids=true | all-gather | bytes 393216 | tf_op jit(solution)/shard_map/all_gather | solution.py:321
  43.9 0.9 shard_map.94
  44.8 2.0 %all-gather.7 = f32[128,512]{1,0:T(8,128)S(1)} all-gather(f32[64,512]{1,0:T(8,128)S(1)} %get-tuple-element.40), channel_id=9, replica_groups={{9,16},{8,0},{11,18},{10,2},{13,20},{12,4},{15,22},{14,6},{24,33},{25,1..., dimensions={0}, use_global_device_ids=true | all-gather | bytes 393216 | tf_op jit(solution)/shard_map/all_gather | solution.py:318
  46.8 2.0 %all-gather.8 = f32[128,512]{1,0:T(8,128)S(1)} all-gather(f32[64,512]{1,0:T(8,128)S(1)} %bitcast_add_fusion.1), channel_id=10, replica_groups=mesh['z'=16,'yhi'=2,'core'=2,'x'=4,'ylo'=2] {'core'}, dimensions={0}, use_global_device_ids=true | all-gather | bytes 393216 | tf_op jit(solution)/shard_map/all_gather | solution.py:321
  48.8 0.9 shard_map.95
  49.7 2.0 %all-gather.9 = f32[128,512]{1,0:T(8,128)S(1)} all-gather(f32[64,512]{1,0:T(8,128)S(1)} %get-tuple-element.42), channel_id=11, replica_groups={{9,16},{8,0},{11,18},{10,2},{13,20},{12,4},{15,22},{14,6},{24,33},{25,1..., dimensions={0}, use_global_device_ids=true | all-gather | bytes 393216 | tf_op jit(solution)/shard_map/all_gather | solution.py:318
  51.7 2.0 %all-gather.10 = f32[128,512]{1,0:T(8,128)S(1)} all-gather(f32[64,512]{1,0:T(8,128)S(1)} %bitcast_add_fusion), channel_id=12, replica_groups=mesh['z'=16,'yhi'=2,'core'=2,'x'=4,'ylo'=2] {'core'}, dimensions={0}, use_global_device_ids=true | all-gather | bytes 393216 | tf_op jit(solution)/shard_map/all_gather | solution.py:321
  53.7 0.9 shard_map.96
  54.6 1.9 %all_gather.95 = f32[2,16,512]{2,1,0:T(8,128)S(1)} all-gather(f32[1,16,512]{2,1,0:T(8,128)S(1)} %dynamic-slice_bitcast_fusion), channel_id=1, replica_groups={{9,16},{8,0},{11,18},{10,2},{13,20},{12,4},{15,22},{14,6},{24,33},{25,1..., dimensions={0}, use_global_device_ids=true | all-gather | bytes 98304 | tf_op jit(solution)/shard_map/all_gather | solution.py:318
  56.5 37.9 %all_gather.96 = f32[4,16,512]{2,1,0:T(8,128)S(1)} all-gather(f32[1,16,512]{2,1,0:T(8,128)S(1)} %bitcast_add_fusion.5), channel_id=1, replica_groups={{0,8,1,9},{2,10,3,11},{4,12,5,13},{6,14,7,15},{16,24,17,25},{18,26,19,2..., dimensions={0}, use_global_device_ids=true | all-gather | bytes 163840 | tf_op jit(solution)/shard_map/all_gather | solution.py:322
  94.4 0.6 bitcast_multiply_fusion
  (8 shorter events, 0.1 us)
Async XLA Ops:
  0.0 17.7 %copy-start.4 = (s32[1,5]{1,0:T(1,128)S(1)}, s32[1,5]{1,0:T(1,128)}, u32[]{:S(2)}) copy-start(s32[1,5]{1,0:T(1,128)} %offsets_hbm.1) | copy-start | bytes 64
  0.0 17.5 %copy-start.1 = (f32[32,32]{1,0:T(8,128)S(1)}, f32[32,32]{1,0:T(8,128)}, u32[]{:S(2)}) copy-start(f32[32,32]{1,0:T(8,128)} %uptake_weight.1) | copy-start | bytes 12292
  0.0 17.6 %copy-start.3 = (f32[32,32]{1,0:T(8,128)S(1)}, f32[32,32]{1,0:T(8,128)}, u32[]{:S(2)}) copy-start(f32[32,32]{1,0:T(8,128)} %param.17) | copy-start | bytes 12292
  0.0 17.7 %copy-start = (f32[16,32,32]{2,1,0:T(8,128)S(1)}, f32[16,32,32]{2,1,0:T(8,128)}, u32[]{:S(2)}) copy-start(f32[16,32,32]{2,1,0:T(8,128)} %inverse.1) | copy-start | bytes 196612
  0.0 17.7 %copy-start.2 = (s32[16]{0:T(128)S(1)}, s32[16]{0:T(128)}, u32[]{:S(2)}) copy-start(s32[16]{0:T(128)} %wet.1) | copy-start | bytes 196
  3.0 25.5 %collective-permute-start = (f32[512,512]{1,0:T(8,128)}, f32[512,512]{1,0:T(8,128)}, u32[]{:S(2)}, u32[]{:S(2)}) collective-permute-start(f32[512,512]{1,0:T(8,128)} %lend.1), channel_id=1, source_target_pairs={{0,8},{8,0},{1,9},{9,1},{2,10},{10,2},{3,11},{11,3},{4,12},{12,4},... | collective-permute-start | bytes 3145736 | tf_op jit(solution)/shard_map/ppermute | solution.py:268
  13.4 12.3 %all-to-all-start = ((f32[8,7,4,512]{3,2,1,0:T(4,128)}), f32[8,7,4,512]{3,2,1,0:T(4,128)S(1)}, u32[]{:S(2)}, u32[]{:S(2)}) async-start(f32[8,7,4,512]{3,2,1,0:T(4,128)} %pack.1), calls=%async_computation | async-start | bytes 917504 | tf_op jit(solution)/shard_map/all_to_all | solution.py:257

commit v2 on v0

--- a/solution.py
+++ b/solution.py
@@ -9,7 +9,7 @@
 REGION = ("z", "yhi", "core")
 TRACER = ("x", "ylo")
 EVERY = REGION + TRACER
-SPAN = 256
+SPAN = 128
 VMEM_LIMIT = 8 * 2**20
 COUNT_AT, CORE_AT = 5, 6
 
@@ -32,7 +32,7 @@
 def chip_groups(sizes):
     nq, nx, ny = sizes
     return [
-        [((q * 2 + core) * nx + x) * ny + ylo for ylo in range(ny) for core in range(2)]
+        [((q * 2 + core) * nx + x) * ny + ylo for ylo in range(ny) for core in (1, 0)]
         for q in range(nq)
         for x in range(nx)
     ]
@@ -311,8 +311,8 @@
     final = lax.all_gather(keep, EVERY, axis_index_groups=chip_groups(sizes))
     joined = 2 * (1 - lax.axis_index("yhi"))
     row = ylo_index * tracers_here
-    mine = lax.dynamic_slice(final, (joined + core_index, row, 0), (1, tracers_here, boxes))[0]
-    theirs = lax.dynamic_slice(final, (joined + 1 - core_index, rows + row, 0), (1, tracers_here, boxes))[0]
+    mine = lax.dynamic_slice(final, (joined + 1 - core_index, row, 0), (1, tracers_here, boxes))[0]
+    theirs = lax.dynamic_slice(final, (joined + core_index, rows + row, 0), (1, tracers_here, boxes))[0]
     return kept[1][0:1] * (mine + theirs)
 
 

time: 95.5 us -> 95.4 us (level)
  no operation moved by 1% of the time
where the time goes in v2:
time: 95.4 us; the launch traced here: 94.9 us
  blocking collectives  62.2 us (65%)
  Pallas kernels  13.1 us (14%)
  starting transfers between devices  12.2 us (13%)
  waiting for transfers between devices  5.6 us (6%)
    all_gather x1, blocking collectives, local(): final = lax.all_gather(keep, EVERY, axis_index_groups=chip_groups(sizes))  37.9 us
    all_gather x6, blocking collectives, local(): arrived = lax.all_gather(send, EVERY, axis_index_groups=groups)  11.8 us
    all_gather x5, blocking collectives, local(): adjoint = lax.all_gather(keep, 'core')  9.97 us
    ppermute x1, starting transfers between devices, local(): borrowed = in_hbm(lax.ppermute(lent, 'core', [(0, 1), (1, 0)]))  8.73 us
    pallas_call x6, Pallas kernels, local(): pl.pallas_call(step, in_specs=[vmem] * 2 + [hbm if first else vmem] + [vm...  5.97 us
    all_to_all x1, waiting for transfers between devices, local(): lax.all_to_all(copies, TRACER, split_axis=0, concat_axis=0, tiled=True)  5.6 us
    all_to_all x1, starting transfers between devices, local(): lax.all_to_all(copies, TRACER, split_axis=0, concat_axis=0, tiled=True)  3.48 us
    pallas_call x1, Pallas kernels, local(): pl.pallas_call(lend_kernel, in_specs=[hbm] * 2, out_specs=vmem, out_shape...  2.91 us
  transfers between devices with their start and end apart: 2, of which 1 were waited for; matrix products, arithmetic and copies ran while one was open for 0% of the time, Pallas kernels for 4%

profile of v2, /device:TPU:1, one launch (start us, length us, event | category | flops | bytes accessed | tf_op | source)
XLA Modules:
  0.0 94.9 jit_solution(4027514867902597134)
XLA Ops:
  0.0 0.0 copy-start.4
  0.0 0.0 copy-start.1
  0.0 0.0 copy-start.3
  0.0 0.0 copy-start
  0.0 0.0 copy-start.2
  0.0 2.9 %lend.1 = f32[512,512]{1,0:T(8,128)} custom-call(s32[1,5]{1,0:T(1,128)} %offsets_hbm.1, bf16[1,5,512,512]{3,2,1,0:T(8,128)(2,1)} %tiles.3), custom_call_target="tpu_custom_call" | custom-call | tf_op jit(solution)/shard_map/lend/pallas_call | solution.py:248
  3.0 8.7 %collective-permute-start = (f32[512,512]{1,0:T(8,128)}, f32[512,512]{1,0:T(8,128)}, u32[]{:S(2)}, u32[]{:S(2)}) collective-permute-start(f32[512,512]{1,0:T(8,128)} %lend.1), channel_id=1, source_target_pairs={{0,8},{8,0},{1,9},{9,1},{2,10},{10,2},{3,11},{11,3},{4,12},{12,4},... | collective-permute-start | bytes 3145736 | tf_op jit(solution)/shard_map/ppermute | solution.py:257
  11.7 1.6 %pack.1 = f32[8,7,4,512]{3,2,1,0:T(4,128)} custom-call(f32[4,512]{1,0:T(4,128)} %cotangent.1, f32[6,4,512]{2,1,0:T(4,128)} %states.1), custom_call_target="tpu_custom_call" | custom-call | tf_op jit(solution)/shard_map/pack/pallas_call | solution.py:237
  13.3 3.5 %all-to-all-start = ((f32[8,7,4,512]{3,2,1,0:T(4,128)}), f32[8,7,4,512]{3,2,1,0:T(4,128)S(1)}, u32[]{:S(2)}, u32[]{:S(2)}) async-start(f32[8,7,4,512]{3,2,1,0:T(4,128)} %pack.1), calls=%async_computation | async-start | bytes 917504 | tf_op jit(solution)/shard_map/all_to_all | solution.py:246
  17.5 0.0 copy-done.1
  17.5 0.1 copy.12
  17.6 0.0 copy-done.3
  17.6 0.1 copy.13
  17.6 0.0 copy-done.4
  17.6 0.1 pad_add_fusion.facts
  17.7 0.0 copy-done
  17.7 0.0 copy-done.2
  17.7 2.3 %arrange.1 = (bf16[4,512,512]{2,1,0:T(8,128)(2,1)S(1)}, f32[40,512]{1,0:T(8,128)S(1)}, f32[8,512]{1,0:T(8,128)S(1)}) custom-call(s32[7]{0:T(128)S(1)} %pad_add_fusion.facts, s32[16]{0:T(128)S(1)} %copy-done.2, bf16[1,5,512,512]{3,2,1,0:T(8,128)(2,1)} %tiles.3, f32[16,32,32]{2,1,0:T(8,128)S(1)} %copy-done), custom_call_target="tpu_custom_call" | custom-call | tf_op jit(solution)/shard_map/arrange/pallas_call | solution.py:258
  20.0 5.6 %all-to-all-done.gathered = f32[8,7,4,512]{3,2,1,0:T(4,128)S(1)} async-done(((f32[8,7,4,512]{3,2,1,0:T(4,128)}), f32[8,7,4,512]{3,2,1,0:T(4,128)S(1)}, u32[]{:S(2)}, u32[]{:S(2)}) %all-to-all-start) | async-done | bytes 458784 | tf_op jit(solution)/shard_map/all_to_all | solution.py:246
  25.6 0.3 gathered.1
  26.0 2.5 %all-gather = f32[144,512]{1,0:T(8,128)S(1)} all-gather(f32[72,512]{1,0:T(8,128)S(1)} %get-tuple-element.26), channel_id=2, replica_groups=mesh['z'=16,'yhi'=2,'core'=2,'x'=4,'ylo'=2] {'core'}, dimensions={0}, use_global_device_ids=true | all-gather | bytes 442368 | tf_op jit(solution)/shard_map/all_gather | solution.py:279
  28.5 0.0 collective-permute-done.refs_2_
  28.5 1.5 %shard_map.91 = (f32[64,512]{1,0:T(8,128)S(1)}, f32[64,512]{1,0:T(8,128)S(1)}, bf16[2,8,128,128]{3,2,1,0:T(8,128)(2,1)S(1)}, f32[4,512]{1,0:T(4,128)S(1)}, bf16[512,512]{1,0:T(8,128)(2,1)S(1)}) custom-call(f32[2,72,512]{2,1,0:T(8,128)S(1)} %bitcast.34, bf16[4,512,512]{2,1,0:T(8,128)(2,1)S(1)} %get-tuple-element.27.refs_1_, ...), custom_call_target="tpu_custom_call" | custom-call | tf_op jit(solution)/shard_map/pallas_call | solution.py:290
  30.0 2.0 %all-gather.1 = f32[128,512]{1,0:T(8,128)S(1)} all-gather(f32[64,512]{1,0:T(8,128)S(1)} %get-tuple-element.32), channel_id=3, replica_groups={{9,16},{8,0},{11,18},{10,2},{13,20},{12,4},{15,22},{14,6},{24,33},{25,1..., dimensions={0}, use_global_device_ids=true | all-gather | bytes 393216 | tf_op jit(solution)/shard_map/all_gather | solution.py:307
  32.0 2.0 %all-gather.2 = f32[128,512]{1,0:T(8,128)S(1)} all-gather(f32[64,512]{1,0:T(8,128)S(1)} %bitcast_add_fusion.4), channel_id=4, replica_groups=mesh['z'=16,'yhi'=2,'core'=2,'x'=4,'ylo'=2] {'core'}, dimensions={0}, use_global_device_ids=true | all-gather | bytes 393216 | tf_op jit(solution)/shard_map/all_gather | solution.py:310
  34.0 0.9 shard_map.92
  34.9 2.0 %all-gather.3 = f32[128,512]{1,0:T(8,128)S(1)} all-gather(f32[64,512]{1,0:T(8,128)S(1)} %get-tuple-element.36), channel_id=5, replica_groups={{9,16},{8,0},{11,18},{10,2},{13,20},{12,4},{15,22},{14,6},{24,33},{25,1..., dimensions={0}, use_global_device_ids=true | all-gather | bytes 393216 | tf_op jit(solution)/shard_map/all_gather | solution.py:307
  36.9 2.0 %all-gather.4 = f32[128,512]{1,0:T(8,128)S(1)} all-gather(f32[64,512]{1,0:T(8,128)S(1)} %bitcast_add_fusion.3), channel_id=6, replica_groups=mesh['z'=16,'yhi'=2,'core'=2,'x'=4,'ylo'=2] {'core'}, dimensions={0}, use_global_device_ids=true | all-gather | bytes 393216 | tf_op jit(solution)/shard_map/all_gather | solution.py:310
  38.9 0.9 shard_map.93
  39.8 2.0 %all-gather.5 = f32[128,512]{1,0:T(8,128)S(1)} all-gather(f32[64,512]{1,0:T(8,128)S(1)} %get-tuple-element.38), channel_id=7, replica_groups={{9,16},{8,0},{11,18},{10,2},{13,20},{12,4},{15,22},{14,6},{24,33},{25,1..., dimensions={0}, use_global_device_ids=true | all-gather | bytes 393216 | tf_op jit(solution)/shard_map/all_gather | solution.py:307
  41.8 2.0 %all-gather.6 = f32[128,512]{1,0:T(8,128)S(1)} all-gather(f32[64,512]{1,0:T(8,128)S(1)} %bitcast_add_fusion.2), channel_id=8, replica_groups=mesh['z'=16,'yhi'=2,'core'=2,'x'=4,'ylo'=2] {'core'}, dimensions={0}, use_global_device_ids=true | all-gather | bytes 393216 | tf_op jit(solution)/shard_map/all_gather | solution.py:310
  43.8 0.9 shard_map.94
  44.7 2.0 %all-gather.7 = f32[128,512]{1,0:T(8,128)S(1)} all-gather(f32[64,512]{1,0:T(8,128)S(1)} %get-tuple-element.40), channel_id=9, replica_groups={{9,16},{8,0},{11,18},{10,2},{13,20},{12,4},{15,22},{14,6},{24,33},{25,1..., dimensions={0}, use_global_device_ids=true | all-gather | bytes 393216 | tf_op jit(solution)/shard_map/all_gather | solution.py:307
  46.7 2.0 %all-gather.8 = f32[128,512]{1,0:T(8,128)S(1)} all-gather(f32[64,512]{1,0:T(8,128)S(1)} %bitcast_add_fusion.1), channel_id=10, replica_groups=mesh['z'=16,'yhi'=2,'core'=2,'x'=4,'ylo'=2] {'core'}, dimensions={0}, use_global_device_ids=true | all-gather | bytes 393216 | tf_op jit(solution)/shard_map/all_gather | solution.py:310
  48.7 0.9 shard_map.95
  49.6 2.0 %all-gather.9 = f32[128,512]{1,0:T(8,128)S(1)} all-gather(f32[64,512]{1,0:T(8,128)S(1)} %get-tuple-element.42), channel_id=11, replica_groups={{9,16},{8,0},{11,18},{10,2},{13,20},{12,4},{15,22},{14,6},{24,33},{25,1..., dimensions={0}, use_global_device_ids=true | all-gather | bytes 393216 | tf_op jit(solution)/shard_map/all_gather | solution.py:307
  51.6 2.0 %all-gather.10 = f32[128,512]{1,0:T(8,128)S(1)} all-gather(f32[64,512]{1,0:T(8,128)S(1)} %bitcast_add_fusion), channel_id=12, replica_groups=mesh['z'=16,'yhi'=2,'core'=2,'x'=4,'ylo'=2] {'core'}, dimensions={0}, use_global_device_ids=true | all-gather | bytes 393216 | tf_op jit(solution)/shard_map/all_gather | solution.py:310
  53.6 0.9 shard_map.96
  54.5 1.9 %all_gather.95 = f32[2,16,512]{2,1,0:T(8,128)S(1)} all-gather(f32[1,16,512]{2,1,0:T(8,128)S(1)} %dynamic-slice_bitcast_fusion), channel_id=1, replica_groups={{9,16},{8,0},{11,18},{10,2},{13,20},{12,4},{15,22},{14,6},{24,33},{25,1..., dimensions={0}, use_global_device_ids=true | all-gather | bytes 98304 | tf_op jit(solution)/shard_map/all_gather | solution.py:307
  56.4 37.9 %all_gather.96 = f32[4,16,512]{2,1,0:T(8,128)S(1)} all-gather(f32[1,16,512]{2,1,0:T(8,128)S(1)} %bitcast_add_fusion.5), channel_id=1, replica_groups={{8,0,9,1},{10,2,11,3},{12,4,13,5},{14,6,15,7},{24,16,25,17},{26,18,27,1..., dimensions={0}, use_global_device_ids=true | all-gather | bytes 163840 | tf_op jit(solution)/shard_map/all_gather | solution.py:311
  94.3 0.6 bitcast_multiply_fusion
  (8 shorter events, 0.1 us)
Async XLA Ops:
  0.0 17.6 %copy-start.4 = (s32[1,5]{1,0:T(1,128)S(1)}, s32[1,5]{1,0:T(1,128)}, u32[]{:S(2)}) copy-start(s32[1,5]{1,0:T(1,128)} %offsets_hbm.1) | copy-start | bytes 64
  0.0 17.5 %copy-start.1 = (f32[32,32]{1,0:T(8,128)S(1)}, f32[32,32]{1,0:T(8,128)}, u32[]{:S(2)}) copy-start(f32[32,32]{1,0:T(8,128)} %uptake_weight.1) | copy-start | bytes 12292
  0.0 17.6 %copy-start.3 = (f32[32,32]{1,0:T(8,128)S(1)}, f32[32,32]{1,0:T(8,128)}, u32[]{:S(2)}) copy-start(f32[32,32]{1,0:T(8,128)} %param.17) | copy-start | bytes 12292
  0.0 17.7 %copy-start = (f32[16,32,32]{2,1,0:T(8,128)S(1)}, f32[16,32,32]{2,1,0:T(8,128)}, u32[]{:S(2)}) copy-start(f32[16,32,32]{2,1,0:T(8,128)} %inverse.1) | copy-start | bytes 196612
  0.0 17.7 %copy-start.2 = (s32[16]{0:T(128)S(1)}, s32[16]{0:T(128)}, u32[]{:S(2)}) copy-start(s32[16]{0:T(128)} %wet.1) | copy-start | bytes 196
  3.0 25.5 %collective-permute-start = (f32[512,512]{1,0:T(8,128)}, f32[512,512]{1,0:T(8,128)}, u32[]{:S(2)}, u32[]{:S(2)}) collective-permute-start(f32[512,512]{1,0:T(8,128)} %lend.1), channel_id=1, source_target_pairs={{0,8},{8,0},{1,9},{9,1},{2,10},{10,2},{3,11},{11,3},{4,12},{12,4},... | collective-permute-start | bytes 3145736 | tf_op jit(solution)/shard_map/ppermute | solution.py:257
  13.3 12.3 %all-to-all-start = ((f32[8,7,4,512]{3,2,1,0:T(4,128)}), f32[8,7,4,512]{3,2,1,0:T(4,128)S(1)}, u32[]{:S(2)}, u32[]{:S(2)}) async-start(f32[8,7,4,512]{3,2,1,0:T(4,128)} %pack.1), calls=%async_computation | async-start | bytes 917504 | tf_op jit(solution)/shard_map/all_to_all | solution.py:246
